TPU v7x, 512 devices: a whole 4x8x8 slice. The times are simulated.
512 devices in a mesh: region: 64 (over z, y), tile: 8 (over x, core).
Axes of the slice: x: 4, y: 8, z: 8, core: 2. Of those that a mesh axis runs over, the one named last changes fastest.
Arguments:
- innovations: float32 [64, 65536], P(None, ('region', 'tile')), may hold values from -6 to 6
- obs_geometry: float32 [3, 65536], P(None, ('region', 'tile')), may hold values from 0 to 35, as said below
- obs_error: float32 [65536], P(('region', 'tile')), may hold values from 0.25 to 1
- tile_owner: int32 [64, 7], P('region'), may hold values from -1 to 7, as said below
Outputs:
- weights: float32 [64, 65536], P(None, ('region', 'tile'))
- residual: float32 [64, 65536], P(None, ('region', 'tile'))
Inputs may be any that keep to these rules, and one draw needn't show every extreme that they name: tile_owner[i, k] names the device along tile that computes the tile of regions i and i + k, or is -1 where that pair is not listed. A region lists the offsets 0 to e - 1 for some e of 1 to 7, and i + k is a region for every listed pair. No device owns more than 4 tiles of its region, and some device owns exactly 4. `obs_geometry`: the standard deviations lie between 0.5 and 2. The operator A built from these positions and the listed tiles is symmetric positive definite.
All inputs are finite; a program needn't handle non-finite values.
Results may differ from a plain program's by a relative error of at most 0.0098.
Values may be sent and summed in bfloat16 or wider, within the bound.
A program may use at most 128 MiB of HBM per device.

v0:
```python
import jax
import jax.numpy as jnp
from jax import lax
from jax.sharding import PartitionSpec as P

ITERS = 2


gc_length = 0.5


def from_behind(block, axis, distance):
    devices = range(lax.axis_size(axis))
    route = [(i - distance, i) for i in devices if i - distance in devices]
    return lax.ppermute(block, axis, route)


def gaspari_cohn(distance):
    scaled = distance / gc_length
    bounded = jnp.maximum(scaled, 1.0)
    near_part = (
        ((-0.25 * scaled + 0.5) * scaled + 0.625) * scaled - 5.0 / 3.0
    ) * scaled * scaled + 1.0
    far_part = (
        ((((scaled / 12.0 - 0.5) * scaled + 0.625) * scaled + 5.0 / 3.0) * scaled - 5.0) * scaled
        + 4.0
        - 2.0 / (3.0 * bounded)
    )
    return jnp.where(scaled <= 1.0, near_part, jnp.where(scaled <= 2.0, far_part, 0.0))


def build_tile(home_rows, far_rows):
    across_x = home_rows[0][:, None] - far_rows[0][None, :]
    across_y = home_rows[1][:, None] - far_rows[1][None, :]
    distance = jnp.sqrt(across_x * across_x + across_y * across_y)
    return (home_rows[2][:, None] * far_rows[2][None, :] * gaspari_cohn(distance)).astype(
        jnp.bfloat16
    )


def empty_tile(home_rows, far_rows):
    return jnp.zeros((home_rows.shape[1], far_rows.shape[1]), jnp.bfloat16)


def home_term(tile_block, far_block):
    return lax.dot_general(
        far_block, tile_block, (((1,), (1,)), ((), ())), preferred_element_type=jnp.float32
    )


def skip_home(tile_block, far_block):
    return jnp.zeros((far_block.shape[0], tile_block.shape[0]), jnp.float32)


def both_terms(tile_block, home_block, far_block):
    to_partner = jnp.dot(home_block, tile_block, preferred_element_type=jnp.float32)
    return (home_term(tile_block, far_block), to_partner)


def skip_both(tile_block, home_block, far_block):
    return (
        skip_home(tile_block, far_block),
        jnp.zeros((home_block.shape[0], tile_block.shape[1]), jnp.float32),
    )


def gram_matrix(left_rows, right_rows):
    return jnp.dot(
        left_rows, right_rows.T, precision=lax.Precision.HIGHEST, preferred_element_type=jnp.float32
    )


def gram_solve(gram_value, target):
    symmetric = 0.5 * (gram_value + gram_value.T)
    factor = jnp.linalg.cholesky(symmetric)
    interim = lax.linalg.triangular_solve(factor, target, left_side=True, lower=True)
    return lax.linalg.triangular_solve(
        factor, interim, left_side=True, lower=True, transpose_a=True
    )


def shards(innovations, obs_geometry, obs_error, tile_owner):
    tile_place = lax.axis_index("tile")
    tile_reach = tile_owner.shape[1]
    owning = tile_owner[0]
    shifted = [obs_geometry]
    for offset in range(1, tile_reach):
        shifted.append(from_behind(obs_geometry, "region", -offset))
    places = lax.all_gather(jnp.stack(shifted), "tile", axis=2, tiled=True)
    owned_flags = []
    tiles = []
    for offset in range(tile_reach):
        is_mine = owning[offset] == tile_place
        owned_flags.append(is_mine)
        tiles.append(lax.cond(is_mine, build_tile, empty_tile, places[0], places[offset]))
    weights = jnp.zeros_like(innovations)
    residual = innovations
    direction = innovations
    squares = lax.psum(gram_matrix(residual, residual), ("region", "tile"))
    for iteration in range(ITERS):
        rounded = direction.astype(jnp.bfloat16)
        pieces = [rounded]
        for apply_offset in range(1, tile_reach):
            pieces.append(from_behind(rounded, "region", -apply_offset))
        blocks = lax.all_gather(jnp.stack(pieces), "tile", axis=2, tiled=True)
        home_total = lax.cond(owned_flags[0], home_term, skip_home, tiles[0], blocks[0])
        outgoing = []
        for apply_offset in range(1, tile_reach):
            to_home, to_partner = lax.cond(
                owned_flags[apply_offset],
                both_terms,
                skip_both,
                tiles[apply_offset],
                blocks[0],
                blocks[apply_offset],
            )
            home_total = home_total + to_home
            outgoing.append(to_partner)
        total_block = home_total
        for apply_offset in range(1, tile_reach):
            total_block = total_block + from_behind(
                outgoing[apply_offset - 1], "region", apply_offset
            )
        summed = lax.psum_scatter(total_block, "tile", scatter_dimension=1, tiled=True)
        image_block = obs_error[None, :] * direction + summed
        curvature = lax.psum(gram_matrix(direction, image_block), ("region", "tile"))
        step_size = gram_solve(curvature, squares)
        weights = weights + jnp.dot(step_size.T, direction, precision=lax.Precision.HIGHEST)
        residual = residual - jnp.dot(step_size.T, image_block, precision=lax.Precision.HIGHEST)
        if iteration + 1 < ITERS:
            next_squares = lax.psum(gram_matrix(residual, residual), ("region", "tile"))
            conjugacy = gram_solve(squares, next_squares)
            direction = residual + jnp.dot(conjugacy.T, direction, precision=lax.Precision.HIGHEST)
            squares = next_squares
    return (weights, residual)


def solution(mesh):
    return jax.shard_map(
        shards,
        mesh=mesh,
        in_specs=(
            P(None, ("region", "tile")),
            P(None, ("region", "tile")),
            P(("region", "tile")),
            P("region", None),
        ),
        out_specs=(P(None, ("region", "tile")), P(None, ("region", "tile"))),
        check_vma=False,
    )
```

profile of v0, /device:TPU:1, one launch (start us, length us, event | category | flops | bytes accessed | tf_op | source)
XLA Modules:
  0.0 742.0 jit_solution(11790609523548990953)
XLA Ops:
  20.5 5.8 collective-permute-done.7
  27.5 7.8 %collective-permute-done.8 = f32[3,128]{1,0:T(4,128)S(1)} collective-permute-done((f32[3,128]{1,0:T(4,128)}, f32[3,128]{1,0:T(4,128)S(1)}, u32[]{:S(2)}, u32[]{:S(2)}) %collective-permute-start.8) | collective-permute-done | bytes 1568 | tf_op jit(solution)/shard_map/ppermute | solution.py:15
  36.6 9.3 %collective-permute-done.9 = f32[3,128]{1,0:T(4,128)S(1)} collective-permute-done((f32[3,128]{1,0:T(4,128)}, f32[3,128]{1,0:T(4,128)S(1)}, u32[]{:S(2)}, u32[]{:S(2)}) %collective-permute-start.9) | collective-permute-done | bytes 1568 | tf_op jit(solution)/shard_map/ppermute | solution.py:15
  47.2 8.6 %collective-permute-done.10 = f32[3,128]{1,0:T(4,128)S(1)} collective-permute-done((f32[3,128]{1,0:T(4,128)}, f32[3,128]{1,0:T(4,128)S(1)}, u32[]{:S(2)}, u32[]{:S(2)}) %collective-permute-start.10) | collective-permute-done | bytes 1568 | tf_op jit(solution)/shard_map/ppermute | solution.py:15
  57.1 8.1 %collective-permute-done.11 = f32[3,128]{1,0:T(4,128)S(1)} collective-permute-done((f32[3,128]{1,0:T(4,128)}, f32[3,128]{1,0:T(4,128)S(1)}, u32[]{:S(2)}, u32[]{:S(2)}) %collective-permute-start.11) | collective-permute-done | bytes 1568 | tf_op jit(solution)/shard_map/ppermute | solution.py:15
  66.6 23.1 %all_gather.10 = f32[7,3,1024]{2,1,0:T(4,128)S(1)} all-gather(f32[7,3,128]{2,1,0:T(4,128)S(1)} %constant_dynamic-update-slice_fusion.7), channel_id=1, replica_groups=mesh['region'=64,'tile'=8] {'tile'}, dimensions={2}, use_global_device_ids=true | all-gather | bytes 96768 | tf_op jit(solution)/shard_map/all_gather | solution.py:89
  91.3 7.9 %collective-permute-done.5 = bf16[64,128]{1,0:T(8,128)(2,1)S(1)} collective-permute-done((bf16[64,128]{1,0:T(8,128)(2,1)S(1)}, bf16[64,128]{1,0:T(8,128)(2,1)S(1)}, u32[]{:S(2)}, u32[]{:S(2)}) %collective-permute-start.5) | collective-permute-done | bytes 16416 | tf_op jit(solution)/shard_map/ppermute | solution.py:15
  99.3 17.0 %all_gather.9 = bf16[7,64,1024]{2,1,0:T(8,128)(2,1)S(1)} all-gather(bf16[7,64,128]{2,1,0:T(8,128)(2,1)S(1)} %constant_dynamic-update-slice_fusion), channel_id=1, replica_groups=mesh['region'=64,'tile'=8] {'tile'}, dimensions={2}, use_global_device_ids=true | all-gather | bytes 1032192 | tf_op jit(solution)/shard_map/all_gather | solution.py:105
  131.4 7.9 %conditional.33 = (bf16[1024,1024]{1,0:T(8,128)(2,1)}) conditional(s32[]{:T(128)} %convert_element_type.69, () %tuple.180, (f32[3,1024]{1,0:T(4,128)S(1)}, f32[7,3,1024]{2,1,0:T(4,128)S(1)}) %tuple.165), branch_computations={%region_24.25_spmd, %region_25.26_spmd} | conditional | flops 37748736 | bytes 2170888 | solution.py:95
  131.5 7.9 %fusion.48 = bf16[1024,1024]{1,0:T(8,128)(2,1)} fusion(f32[1024]{0:T(1024)S(1)} %bitcast.280, f32[1024]{0:T(1024)S(1)} %bitcast.262, f32[1024]{0:T(1024)S(1)} %bitcast.281, f32[1024]{0:T(1024)S(1)} %bitcast.263, f32[1024]{0:T(1024)S(1)} %bitcast.279, f32[1024]{0:T(1024)S(1)} %bitcast.261), kind=kLoop, calls=%fused_computation.73 | loop fusion | flops 37748736 | bytes 2121728 | tf_op jit(solution)/shard_map/cond/branch_1_fun/convert_element_type | solution.py:36
  142.8 20.0 %collective-permute-start.14 = (f32[64,1024]{1,0:T(8,128)}, f32[64,1024]{1,0:T(8,128)}, u32[]{:S(2)}, u32[]{:S(2)}) collective-permute-start(f32[64,1024]{1,0:T(8,128)} %get-tuple-element.258), channel_id=1, source_target_pairs={{0,24},{8,32},{16,40},{24,48},{32,56},{40,64},{48,72},{56,80},{64,... | collective-permute-start | bytes 786440 | tf_op jit(solution)/shard_map/ppermute | solution.py:15
  174.4 10.8 %collective-permute-start.17 = (f32[64,1024]{1,0:T(8,128)}, f32[64,1024]{1,0:T(8,128)}, u32[]{:S(2)}, u32[]{:S(2)}) collective-permute-start(f32[64,1024]{1,0:T(8,128)} %get-tuple-element.261), channel_id=1, source_target_pairs={{0,48},{8,56},{16,64},{24,72},{32,80},{40,88},{48,96},{56,104},{64... | collective-permute-start | bytes 786440 | tf_op jit(solution)/shard_map/ppermute | solution.py:15
  188.2 10.9 %collective-permute-done.16 = f32[64,1024]{1,0:T(8,128)} collective-permute-done((f32[64,1024]{1,0:T(8,128)}, f32[64,1024]{1,0:T(8,128)}, u32[]{:S(2)}, u32[]{:S(2)}) %collective-permute-start.16) | collective-permute-done | bytes 262176 | tf_op jit(solution)/shard_map/ppermute | solution.py:15
  199.1 5.8 collective-permute-done.17
  207.6 47.2 %reduce-scatter.3.cloned.1.call-done = f32[64,128]{1,0:T(8,128)} async-done(((f32[64,1024]{1,0:T(8,128)}), f32[64,128]{1,0:T(8,128)}) %reduce-scatter.3.cloned.1.call-update) | async-done | bytes 32784 | tf_op jit(solution)/shard_map/reduce_scatter | solution.py:124
  255.8 99.7 %all-reduce = (f32[64,64]{1,0:T(8,128)S(1)}, f32[64,64]{1,0:T(8,128)S(1)}) all-reduce(f32[64,64]{1,0:T(8,128)S(1)} %fusion.125, f32[64,64]{1,0:T(8,128)S(1)} %convolution_bitcast_fusion), channel_id=1, replica_groups=mesh['region'=64,'tile'=8] {'region','tile'}, use_global_device_ids=true, to_apply=%region_32.34 | all-reduce | flops 8192 | bytes 65536 | tf_op jit(solution)/shard_map/psum | solution.py:99
  355.8 5.8 cholesky.70
  363.0 4.9 custom-call.15
  368.0 5.8 cholesky.59
  375.1 4.9 custom-call.13
  381.7 94.6 %psum.30 = f32[64,64]{1,0:T(8,128)S(1)} all-reduce(f32[64,64]{1,0:T(8,128)S(1)} %fusion.127), channel_id=1, replica_groups=mesh['region'=64,'tile'=8] {'region','tile'}, use_global_device_ids=true, to_apply=%region_33.0 | all-reduce | flops 4096 | bytes 32768 | tf_op jit(solution)/shard_map/psum | solution.py:131
  495.5 16.3 %all_gather.11 = bf16[7,64,1024]{2,1,0:T(8,128)(2,1)S(1)} all-gather(bf16[7,64,128]{2,1,0:T(8,128)(2,1)S(1)} %constant_dynamic-update-slice_fusion.14), channel_id=1, replica_groups=mesh['region'=64,'tile'=8] {'tile'}, dimensions={2}, use_global_device_ids=true | all-gather | bytes 1032192 | tf_op jit(solution)/shard_map/all_gather | solution.py:105
  517.2 5.0 collective-permute-start.25
  523.0 9.2 %collective-permute-start.26 = (f32[64,1024]{1,0:T(8,128)}, f32[64,1024]{1,0:T(8,128)}, u32[]{:S(2)}, u32[]{:S(2)}) collective-permute-start(f32[64,1024]{1,0:T(8,128)} %get-tuple-element.270), channel_id=1, source_target_pairs={{0,24},{8,32},{16,40},{24,48},{32,56},{40,64},{48,72},{56,80},{64,... | collective-permute-start | bytes 786440 | tf_op jit(solution)/shard_map/ppermute | solution.py:15
  533.0 6.3 collective-permute-start.27
  540.0 6.8 collective-permute-start.28
  557.0 6.9 collective-permute-done.28
  563.9 14.7 %collective-permute-done.29 = f32[64,1024]{1,0:T(8,128)S(1)} collective-permute-done((f32[64,1024]{1,0:T(8,128)}, f32[64,1024]{1,0:T(8,128)S(1)}, u32[]{:S(2)}, u32[]{:S(2)}) %collective-permute-start.29) | collective-permute-done | bytes 262176 | tf_op jit(solution)/shard_map/ppermute | solution.py:15
  581.1 38.1 %reduce-scatter.5.cloned.1.call-done = f32[64,128]{1,0:T(8,128)} async-done(((f32[64,1024]{1,0:T(8,128)}), f32[64,128]{1,0:T(8,128)}) %reduce-scatter.5.cloned.1.call-update) | async-done | bytes 32784 | tf_op jit(solution)/shard_map/reduce_scatter | solution.py:124
  620.2 99.4 %psum.31 = f32[64,64]{1,0:T(8,128)S(1)} all-reduce(f32[64,64]{1,0:T(8,128)S(1)} %fusion.92), channel_id=1, replica_groups=mesh['region'=64,'tile'=8] {'region','tile'}, use_global_device_ids=true, to_apply=%region_49.53 | all-reduce | flops 4096 | bytes 32768 | tf_op jit(solution)/shard_map/psum | solution.py:126
  719.8 5.8 cholesky.81
  726.9 4.9 custom-call.17
  (207 shorter events, 127.4 us)
Async XLA Ops:
  7.2 247.7 %reduce-scatter.3.cloned.1.call-start = ((), (), s32[]{:S(2)}) async-start(), calls=%async_computation.2 | async-start | bytes 294912 | tf_op jit(solution)/shard_map/reduce_scatter | solution.py:124
  8.0 82.0 %collective-permute-start = (bf16[64,128]{1,0:T(8,128)(2,1)S(1)}, bf16[64,128]{1,0:T(8,128)(2,1)S(1)}, u32[]{:S(2)}, u32[]{:S(2)}) collective-permute-start(bf16[64,128]{1,0:T(8,128)(2,1)S(1)} %get-tuple-element.279), channel_id=1, source_target_pairs={{8,0},{16,8},{24,16},{32,24},{40,32},{48,40},{56,48},{64,56},{72,6... | collective-permute-start | bytes 49160 | tf_op jit(solution)/shard_map/ppermute | solution.py:15
  9.3 82.0 %collective-permute-start.1 = (bf16[64,128]{1,0:T(8,128)(2,1)S(1)}, bf16[64,128]{1,0:T(8,128)(2,1)S(1)}, u32[]{:S(2)}, u32[]{:S(2)}) collective-permute-start(bf16[64,128]{1,0:T(8,128)(2,1)S(1)} %get-tuple-element.279), channel_id=1, source_target_pairs={{16,0},{24,8},{32,16},{40,24},{48,32},{56,40},{64,48},{72,56},{80,... | collective-permute-start | bytes 49160 | tf_op jit(solution)/shard_map/ppermute | solution.py:15
  10.6 80.7 %collective-permute-start.2 = (bf16[64,128]{1,0:T(8,128)(2,1)S(1)}, bf16[64,128]{1,0:T(8,128)(2,1)S(1)}, u32[]{:S(2)}, u32[]{:S(2)}) collective-permute-start(bf16[64,128]{1,0:T(8,128)(2,1)S(1)} %get-tuple-element.279), channel_id=1, source_target_pairs={{24,0},{32,8},{40,16},{48,24},{56,32},{64,40},{72,48},{80,56},{88,... | collective-permute-start | bytes 49160 | tf_op jit(solution)/shard_map/ppermute | solution.py:15
  11.9 79.4 %collective-permute-start.3 = (bf16[64,128]{1,0:T(8,128)(2,1)S(1)}, bf16[64,128]{1,0:T(8,128)(2,1)S(1)}, u32[]{:S(2)}, u32[]{:S(2)}) collective-permute-start(bf16[64,128]{1,0:T(8,128)(2,1)S(1)} %get-tuple-element.279), channel_id=1, source_target_pairs={{32,0},{40,8},{48,16},{56,24},{64,32},{72,40},{80,48},{88,56},{96,... | collective-permute-start | bytes 49160 | tf_op jit(solution)/shard_map/ppermute | solution.py:15
  13.2 6.0 collective-permute-start.6
  19.2 7.1 collective-permute-start.7
  26.2 9.1 %collective-permute-start.8 = (f32[3,128]{1,0:T(4,128)}, f32[3,128]{1,0:T(4,128)S(1)}, u32[]{:S(2)}, u32[]{:S(2)}) collective-permute-start(f32[3,128]{1,0:T(4,128)} %param.52), channel_id=1, source_target_pairs={{24,0},{32,8},{40,16},{48,24},{56,32},{64,40},{72,48},{80,56},{88,... | collective-permute-start | bytes 4616 | tf_op jit(solution)/shard_map/ppermute | solution.py:15
  35.3 10.6 %collective-permute-start.9 = (f32[3,128]{1,0:T(4,128)}, f32[3,128]{1,0:T(4,128)S(1)}, u32[]{:S(2)}, u32[]{:S(2)}) collective-permute-start(f32[3,128]{1,0:T(4,128)} %param.52), channel_id=1, source_target_pairs={{32,0},{40,8},{48,16},{56,24},{64,32},{72,40},{80,48},{88,56},{96,... | collective-permute-start | bytes 4616 | tf_op jit(solution)/shard_map/ppermute | solution.py:15
  45.9 9.9 %collective-permute-start.10 = (f32[3,128]{1,0:T(4,128)}, f32[3,128]{1,0:T(4,128)S(1)}, u32[]{:S(2)}, u32[]{:S(2)}) collective-permute-start(f32[3,128]{1,0:T(4,128)} %param.52), channel_id=1, source_target_pairs={{40,0},{48,8},{56,16},{64,24},{72,32},{80,40},{88,48},{96,56},{104... | collective-permute-start | bytes 4616 | tf_op jit(solution)/shard_map/ppermute | solution.py:15
  55.8 9.4 %collective-permute-start.11 = (f32[3,128]{1,0:T(4,128)}, f32[3,128]{1,0:T(4,128)S(1)}, u32[]{:S(2)}, u32[]{:S(2)}) collective-permute-start(f32[3,128]{1,0:T(4,128)} %param.52), channel_id=1, source_target_pairs={{48,0},{56,8},{64,16},{72,24},{80,32},{88,40},{96,48},{104,56},{11... | collective-permute-start | bytes 4616 | tf_op jit(solution)/shard_map/ppermute | solution.py:15
  65.3 26.0 %collective-permute-start.4 = (bf16[64,128]{1,0:T(8,128)(2,1)S(1)}, bf16[64,128]{1,0:T(8,128)(2,1)S(1)}, u32[]{:S(2)}, u32[]{:S(2)}) collective-permute-start(bf16[64,128]{1,0:T(8,128)(2,1)S(1)} %get-tuple-element.279), channel_id=1, source_target_pairs={{40,0},{48,8},{56,16},{64,24},{72,32},{80,40},{88,48},{96,56},{104... | collective-permute-start | bytes 49160 | tf_op jit(solution)/shard_map/ppermute | solution.py:15
  89.9 9.3 %collective-permute-start.5 = (bf16[64,128]{1,0:T(8,128)(2,1)S(1)}, bf16[64,128]{1,0:T(8,128)(2,1)S(1)}, u32[]{:S(2)}, u32[]{:S(2)}) collective-permute-start(bf16[64,128]{1,0:T(8,128)(2,1)S(1)} %get-tuple-element.279), channel_id=1, source_target_pairs={{48,0},{56,8},{64,16},{72,24},{80,32},{88,40},{96,48},{104,56},{11... | collective-permute-start | bytes 49160 | tf_op jit(solution)/shard_map/ppermute | solution.py:15
  117.1 57.3 %collective-permute-start.12 = (f32[64,1024]{1,0:T(8,128)}, f32[64,1024]{1,0:T(8,128)}, u32[]{:S(2)}, u32[]{:S(2)}) collective-permute-start(f32[64,1024]{1,0:T(8,128)} %get-tuple-element.256), channel_id=1, source_target_pairs={{0,8},{8,16},{16,24},{24,32},{32,40},{40,48},{48,56},{56,64},{64,7... | collective-permute-start | bytes 786440 | tf_op jit(solution)/shard_map/ppermute | solution.py:15
  140.1 48.1 %collective-permute-start.13 = (f32[64,1024]{1,0:T(8,128)}, f32[64,1024]{1,0:T(8,128)}, u32[]{:S(2)}, u32[]{:S(2)}) collective-permute-start(f32[64,1024]{1,0:T(8,128)} %get-tuple-element.257), channel_id=1, source_target_pairs={{0,16},{8,24},{16,32},{24,40},{32,48},{40,56},{48,64},{56,72},{64,... | collective-permute-start | bytes 786440 | tf_op jit(solution)/shard_map/ppermute | solution.py:15
  142.8 45.4 %collective-permute-start.14 = (f32[64,1024]{1,0:T(8,128)}, f32[64,1024]{1,0:T(8,128)}, u32[]{:S(2)}, u32[]{:S(2)}) collective-permute-start(f32[64,1024]{1,0:T(8,128)} %get-tuple-element.258), channel_id=1, source_target_pairs={{0,24},{8,32},{16,40},{24,48},{32,56},{40,64},{48,72},{56,80},{64,... | collective-permute-start | bytes 786440 | tf_op jit(solution)/shard_map/ppermute | solution.py:15
  163.6 24.6 %collective-permute-start.15 = (f32[64,1024]{1,0:T(8,128)}, f32[64,1024]{1,0:T(8,128)}, u32[]{:S(2)}, u32[]{:S(2)}) collective-permute-start(f32[64,1024]{1,0:T(8,128)} %get-tuple-element.259), channel_id=1, source_target_pairs={{0,32},{8,40},{16,48},{24,56},{32,64},{40,72},{48,80},{56,88},{64,... | collective-permute-start | bytes 786440 | tf_op jit(solution)/shard_map/ppermute | solution.py:15
  166.3 32.7 %collective-permute-start.16 = (f32[64,1024]{1,0:T(8,128)}, f32[64,1024]{1,0:T(8,128)}, u32[]{:S(2)}, u32[]{:S(2)}) collective-permute-start(f32[64,1024]{1,0:T(8,128)} %get-tuple-element.260), channel_id=1, source_target_pairs={{0,40},{8,48},{16,56},{24,64},{32,72},{40,80},{48,88},{56,96},{64,... | collective-permute-start | bytes 786440 | tf_op jit(solution)/shard_map/ppermute | solution.py:15
  174.4 30.4 %collective-permute-start.17 = (f32[64,1024]{1,0:T(8,128)}, f32[64,1024]{1,0:T(8,128)}, u32[]{:S(2)}, u32[]{:S(2)}) collective-permute-start(f32[64,1024]{1,0:T(8,128)} %get-tuple-element.261), channel_id=1, source_target_pairs={{0,48},{8,56},{16,64},{24,72},{32,80},{40,88},{48,96},{56,104},{64... | collective-permute-start | bytes 786440 | tf_op jit(solution)/shard_map/ppermute | solution.py:15
  207.4 411.8 %reduce-scatter.5.cloned.1.call-start = ((), (), s32[]{:S(2)}) async-start(), calls=%async_computation.3 | async-start | bytes 294912 | tf_op jit(solution)/shard_map/reduce_scatter | solution.py:124
  476.9 6.5 collective-permute-start.18
  478.2 6.5 collective-permute-start.19
  479.5 7.8 %collective-permute-start.20 = (bf16[64,128]{1,0:T(8,128)(2,1)S(1)}, bf16[64,128]{1,0:T(8,128)(2,1)S(1)}, u32[]{:S(2)}, u32[]{:S(2)}) collective-permute-start(bf16[64,128]{1,0:T(8,128)(2,1)S(1)} %get-tuple-element.277), channel_id=1, source_target_pairs={{24,0},{32,8},{40,16},{48,24},{56,32},{64,40},{72,48},{80,56},{88,... | collective-permute-start | bytes 49160 | tf_op jit(solution)/shard_map/ppermute | solution.py:15
  480.8 10.2 %collective-permute-start.21 = (bf16[64,128]{1,0:T(8,128)(2,1)S(1)}, bf16[64,128]{1,0:T(8,128)(2,1)S(1)}, u32[]{:S(2)}, u32[]{:S(2)}) collective-permute-start(bf16[64,128]{1,0:T(8,128)(2,1)S(1)} %get-tuple-element.277), channel_id=1, source_target_pairs={{32,0},{40,8},{48,16},{56,24},{64,32},{72,40},{80,48},{88,56},{96,... | collective-permute-start | bytes 49160 | tf_op jit(solution)/shard_map/ppermute | solution.py:15
  482.1 10.8 %collective-permute-start.22 = (bf16[64,128]{1,0:T(8,128)(2,1)S(1)}, bf16[64,128]{1,0:T(8,128)(2,1)S(1)}, u32[]{:S(2)}, u32[]{:S(2)}) collective-permute-start(bf16[64,128]{1,0:T(8,128)(2,1)S(1)} %get-tuple-element.277), channel_id=1, source_target_pairs={{40,0},{48,8},{56,16},{64,24},{72,32},{80,40},{88,48},{96,56},{104... | collective-permute-start | bytes 49160 | tf_op jit(solution)/shard_map/ppermute | solution.py:15
  483.4 12.1 %collective-permute-start.23 = (bf16[64,128]{1,0:T(8,128)(2,1)S(1)}, bf16[64,128]{1,0:T(8,128)(2,1)S(1)}, u32[]{:S(2)}, u32[]{:S(2)}) collective-permute-start(bf16[64,128]{1,0:T(8,128)(2,1)S(1)} %get-tuple-element.277), channel_id=1, source_target_pairs={{48,0},{56,8},{64,16},{72,24},{80,32},{88,40},{96,48},{104,56},{11... | collective-permute-start | bytes 49160 | tf_op jit(solution)/shard_map/ppermute | solution.py:15
  512.5 38.3 %collective-permute-start.24 = (f32[64,1024]{1,0:T(8,128)}, f32[64,1024]{1,0:T(8,128)}, u32[]{:S(2)}, u32[]{:S(2)}) collective-permute-start(f32[64,1024]{1,0:T(8,128)} %get-tuple-element.268), channel_id=1, source_target_pairs={{0,8},{8,16},{16,24},{24,32},{32,40},{40,48},{48,56},{56,64},{64,7... | collective-permute-start | bytes 786440 | tf_op jit(solution)/shard_map/ppermute | solution.py:15
  517.2 36.5 %collective-permute-start.25 = (f32[64,1024]{1,0:T(8,128)}, f32[64,1024]{1,0:T(8,128)}, u32[]{:S(2)}, u32[]{:S(2)}) collective-permute-start(f32[64,1024]{1,0:T(8,128)} %get-tuple-element.269), channel_id=1, source_target_pairs={{0,16},{8,24},{16,32},{24,40},{32,48},{40,56},{48,64},{56,72},{64,... | collective-permute-start | bytes 786440 | tf_op jit(solution)/shard_map/ppermute | solution.py:15
  523.0 30.8 %collective-permute-start.26 = (f32[64,1024]{1,0:T(8,128)}, f32[64,1024]{1,0:T(8,128)}, u32[]{:S(2)}, u32[]{:S(2)}) collective-permute-start(f32[64,1024]{1,0:T(8,128)} %get-tuple-element.270), channel_id=1, source_target_pairs={{0,24},{8,32},{16,40},{24,48},{32,56},{40,64},{48,72},{56,80},{64,... | collective-permute-start | bytes 786440 | tf_op jit(solution)/shard_map/ppermute | solution.py:15
  533.0 24.0 %collective-permute-start.27 = (f32[64,1024]{1,0:T(8,128)}, f32[64,1024]{1,0:T(8,128)}, u32[]{:S(2)}, u32[]{:S(2)}) collective-permute-start(f32[64,1024]{1,0:T(8,128)} %get-tuple-element.271), channel_id=1, source_target_pairs={{0,32},{8,40},{16,48},{24,56},{32,64},{40,72},{48,80},{56,88},{64,... | collective-permute-start | bytes 786440 | tf_op jit(solution)/shard_map/ppermute | solution.py:15
  540.0 23.8 %collective-permute-start.28 = (f32[64,1024]{1,0:T(8,128)}, f32[64,1024]{1,0:T(8,128)}, u32[]{:S(2)}, u32[]{:S(2)}) collective-permute-start(f32[64,1024]{1,0:T(8,128)} %get-tuple-element.272), channel_id=1, source_target_pairs={{0,40},{8,48},{16,56},{24,64},{32,72},{40,80},{48,88},{56,96},{64,... | collective-permute-start | bytes 786440 | tf_op jit(solution)/shard_map/ppermute | solution.py:15
  550.8 27.7 %collective-permute-start.29 = (f32[64,1024]{1,0:T(8,128)}, f32[64,1024]{1,0:T(8,128)S(1)}, u32[]{:S(2)}, u32[]{:S(2)}) collective-permute-start(f32[64,1024]{1,0:T(8,128)} %get-tuple-element.273), channel_id=1, source_target_pairs={{0,48},{8,56},{16,64},{24,72},{32,80},{40,88},{48,96},{56,104},{64... | collective-permute-start | bytes 786440 | tf_op jit(solution)/shard_map/ppermute | solution.py:15
  (22 other events, 471.5 us)
Sparse Core Ops, SparseCore 0:
  207.5 47.3 reduce-scatter.2
  581.0 38.1 reduce-scatter.4
where the time goes:
time: 750 us; the launch traced here: 742 us
  blocking collectives  350 us (47%)
  waiting for transfers between devices  187 us (25%)
  starting transfers between devices  100 us (13%)
  other arithmetic  49.8 us (7%)
  between operations  19.7 us (3%)
  local copies, waits for them, and re-layouts  19.4 us (3%)
  matrix products  15.5 us (2%)
    ppermute x30, waiting for transfers between devices, from_behind(): return lax.ppermute(block, axis, route)  101 us
    ppermute x30, starting transfers between devices, from_behind(): return lax.ppermute(block, axis, route)  100 us
    psum x1, blocking collectives, shards(): squares = lax.psum(gram_matrix(residual, residual), ('region', 'tile'))  99.7 us
    psum x1, blocking collectives, shards(): lax.psum(gram_matrix(direction, image_block), ('region', 'tile'))  99.4 us
    psum x1, blocking collectives, shards(): next_squares = lax.psum(gram_matrix(residual, residual), ('region', 'tile'))  94.6 us
    reduce_scatter x2, waiting for transfers between devices, shards(): lax.psum_scatter(total_block, 'tile', scatter_dimension=1, tiled=True)  85.3 us
    all_gather x2, blocking collectives, shards(): blocks = lax.all_gather(jnp.stack(pieces), 'tile', axis=2, tiled=True)  33.3 us
    all_gather x1, blocking collectives, shards(): places = lax.all_gather(jnp.stack(shifted), 'tile', axis=2, tiled=True)  23.1 us
  transfers between devices with their start and end apart: 32, of which 18 were waited for; matrix products, arithmetic and copies ran while one was open for 5% of the time, Pallas kernels for 0%

commit v1 on v0

v1 whole, which is shorter than its diff:
```python
import functools

import jax
import jax.numpy as jnp
from jax import lax
from jax.experimental import pallas as pl
from jax.experimental.pallas import tpu as pltpu
from jax.sharding import PartitionSpec as P

MESH = pl.DeviceIdType.MESH
F32 = jnp.float32
BF16 = jnp.bfloat16
HI = lax.Precision.HIGHEST
LANES = 128


def dot_nn(a, b):
    return lax.dot_general(a, b, (((1,), (0,)), ((), ())), precision=HI, preferred_element_type=F32)


def dot_nt(a, b):
    return lax.dot_general(a, b, (((1,), (1,)), ((), ())), precision=HI, preferred_element_type=F32)


def eliminate(matrix, target):
    n = matrix.shape[0]
    work = jnp.concatenate([matrix, target], axis=1)
    rows = lax.broadcasted_iota(jnp.int32, (n, 1), 0)
    for k in range(n):
        row = work[k : k + 1, :] * (1.0 / work[k : k + 1, k : k + 1])
        work = jnp.where(rows == k, row, work - work[:, k : k + 1] * row)
    return work[:, n:]


def tile_block(x_far, y_far, s_far, x_home, y_home, s_home):
    dx = x_far - x_home
    dy = y_far - y_home
    square = jnp.maximum(dx * dx + dy * dy, 1e-30)
    inverse = lax.rsqrt(square)
    z = square * inverse
    near = ((((-0.25 * z + 0.5) * z + 0.625) * z) - 5.0 / 3.0) * square + 1.0
    rest = jnp.maximum(2.0 - z, 0.0)
    rest2 = rest * rest
    far = rest2 * rest2 * ((z * (1.0 / 12.0) + 1.0 / 6.0) - inverse * (1.0 / 24.0))
    return (s_far * s_home) * jnp.where(z <= 1.0, near, far)


class Exchange:
    def __init__(self, send_sems, recv_sems, base):
        self.send_sems, self.recv_sems, self.base = send_sems, recv_sems, base

    def copy(self, src, dst, index, device):
        return pltpu.make_async_remote_copy(
            src_ref=src,
            dst_ref=dst,
            send_sem=self.send_sems.at[self.base + index],
            recv_sem=self.recv_sems.at[self.base + index],
            device_id=device,
            device_id_type=MESH,
        )


def kernel(
    cfg, v0_ref, geo_ref, err_ref, own_ref, w_ref, r_ref,
    pb, hb, xb, yb, sb, ub0, ub1, cb, acc0, acc1, rs0, rs1, v1_ref, v2_ref, basis,
    l1, t1, y1, z1, g1, l2, t2, y2, z2, g2, send_sems, recv_sems,
):
    R, T, NY, REACH = cfg
    NZ = R // NY
    S = 2 * REACH - 1
    n = v0_ref.shape[0]
    mid = REACH - 1
    r = lax.axis_index("region")
    t = lax.axis_index("tile")
    y = lax.rem(r, NY)
    z = lax.div(r, NY)
    offsets = [d for k in range(1, REACH) for d in (k, -k)]

    def region(d):
        return (lax.rem(r + d + R, R), t)

    def along_tile(o):
        return (r, lax.rem(t + o, T))

    def along_y(o):
        return (z * NY + lax.rem(y + o, NY), t)

    def along_z(o):
        return (lax.rem(z + o, NZ) * NY + y, t)

    peers = [region(d) for d in offsets] + [along_tile(o) for o in range(1, T)]
    peers += [along_y(o) for o in range(1, NY)] + [along_z(o) for o in range(1, NZ)]

    barrier = pltpu.get_barrier_semaphore()
    for peer in peers:
        pl.semaphore_signal(barrier, inc=1, device_id=peer, device_id_type=MESH)

    base = [0]

    def stage(count):
        made = Exchange(send_sems, recv_sems, base[0])
        base[0] += count
        return made

    pb[mid, 0:2, :] = geo_ref[0:2, :] * 2.0
    pb[mid, 2:3, :] = geo_ref[2:3, :]
    pb[mid, 3:4, :] = jnp.zeros((1, LANES), F32)
    pb[mid, 3:4, 0:REACH] = jnp.where(own_ref[0:1, :] >= 0, 1.0, 0.0)
    pb[mid, 4:8, :] = jnp.zeros((4, LANES), F32)
    hb[0] = pb[mid]
    ub0[mid] = v0_ref[...].astype(BF16)

    pl.semaphore_wait(barrier, len(peers))

    geo_stage, home_stage, u0_stage = stage(len(offsets)), stage(T - 1), stage(len(offsets))
    sends = []
    for index, d in enumerate(offsets):
        sends.append(geo_stage.copy(pb.at[mid], pb.at[mid - d], index, region(d)))
    for o in range(1, T):
        sends.append(home_stage.copy(hb.at[0], hb.at[o], o - 1, along_tile(o)))
    for index, d in enumerate(offsets):
        sends.append(u0_stage.copy(ub0.at[mid], ub0.at[mid - d], index, region(d)))
    for copy in sends:
        copy.start()
    for copy in sends[: len(offsets) + T - 1]:
        copy.wait_recv()

    for s in range(S):
        block = pb[s]
        d = s - mid
        listed = pb[mid if d >= 0 else s, 3:4, abs(d) : abs(d) + 1]
        columns = block.T
        xb[s] = jnp.broadcast_to(columns[:, 0:1], (LANES, LANES))
        yb[s] = jnp.broadcast_to(columns[:, 1:2], (LANES, LANES))
        sb[s] = jnp.broadcast_to(columns[:, 2:3] * listed, (LANES, LANES))

    def build(step, carry):
        for o in range(T):
            home = hb[o]
            block = tile_block(xb[step], yb[step], sb[step], home[0:1, :], home[1:2, :], home[2:3, :])
            cb[o, step] = block.astype(BF16)
        return carry

    lax.fori_loop(0, S, build, 0)

    def apply(ub, acc, rs, v_ref, out_ref):
        found = stage(T - 1)
        whole = jnp.concatenate([ub[s] for s in range(S)], axis=1)

        def out_copy(o):
            return found.copy(acc.at[o], rs.at[o - 1], o - 1, (r, lax.rem(t - o + T, T)))

        def product(step, carry):
            o = lax.rem(step + 1, T)
            acc[o] = jnp.dot(whole, cb[o].reshape(S * LANES, LANES), preferred_element_type=F32)

            @pl.when(step >= 1)
            def _():
                out_copy(step).start()

            return carry

        lax.fori_loop(0, T, product, 0)
        total = err_ref[...] * v_ref[...] + acc[0]
        for o in range(1, T):
            copy = out_copy(o)
            copy.wait_recv()
            total = total + rs[o - 1]
            sends.append(copy)
        out_ref[...] = total

    for copy in sends[len(offsets) + T - 1 :]:
        copy.wait_recv()
    apply(ub0, acc0, rs0, v0_ref, v1_ref)

    ub1[mid] = v1_ref[...].astype(BF16)
    u1_stage = stage(len(offsets))
    u1_copies = [u1_stage.copy(ub1.at[mid], ub1.at[mid - d], index, region(d)) for index, d in enumerate(offsets)]

    class Sum:
        def __init__(self, local, tile_part, y_part, z_part, result):
            self.local, self.parts, self.result = local, (tile_part, y_part, z_part), result
            self.stages = [stage(T - 1), stage(NY - 1), stage(NZ - 1), stage(T - 1)]
            self.pending = []

        def start(self, copies):
            for copy in copies:
                copy.start()
            self.pending = copies
            sends.extend(copies)

        def wait(self):
            for copy in self.pending:
                copy.wait_recv()

        def send_tile(self):
            self.parts[0][t] = self.local[t]
            self.start([
                self.stages[0].copy(self.local.at[lax.rem(t + o, T)], self.parts[0].at[t], o - 1, along_tile(o))
                for o in range(1, T)
            ])

        def total(self, part, count):
            self.wait()
            value = part[0]
            for i in range(1, count):
                value = value + part[i]
            return value

        def send_y(self):
            self.parts[1][y] = self.total(self.parts[0], T)
            part = self.parts[1].at[y]
            self.start([self.stages[1].copy(part, part, o - 1, along_y(o)) for o in range(1, NY)])

        def send_z(self):
            self.parts[2][z] = self.total(self.parts[1], NY)
            part = self.parts[2].at[z]
            self.start([self.stages[2].copy(part, part, o - 1, along_z(o)) for o in range(1, NZ)])

        def send_result(self):
            self.result[t] = self.total(self.parts[2], NZ)
            part = self.result.at[t]
            self.start([self.stages[3].copy(part, part, o - 1, along_tile(o)) for o in range(1, T)])

        def finish(self):
            self.wait()
            return self.result[...].reshape(-1, LANES)

    first = Sum(l1, t1, y1, z1, g1)
    second = Sum(l2, t2, y2, z2, g2)

    for copy in u1_copies:
        copy.start()
        sends.append(copy)
    basis[:n, :LANES] = v0_ref[...]
    basis[n:, :LANES] = v1_ref[...]
    basis[:n, LANES:] = v1_ref[...]
    both = basis[:, :LANES]
    l1[...] = dot_nt(both, both).reshape(l1.shape)
    first.send_tile()
    first.send_y()
    for copy in u1_copies:
        copy.wait_recv()
    apply(ub1, acc1, rs1, v1_ref, v2_ref)
    l2[...] = dot_nt(v2_ref[...], both).reshape(l2.shape)
    second.send_tile()
    first.send_z()
    second.send_y()
    first.send_result()

    v0, v1, v2 = v0_ref[...], v1_ref[...], v2_ref[...]
    gram = first.finish()
    g00, g01, g10, g11 = gram[:n, :n], gram[:n, n:], gram[n:, :n], gram[n:, n:]
    step1 = eliminate(0.5 * (g01 + g01.T), g00)
    next_squares = (g00 - dot_nn(g01, step1)) - dot_nn(step1.T, g10 - dot_nn(g11, step1))
    conjugacy = eliminate(0.5 * (g00 + g00.T), next_squares)
    eye = (
        lax.broadcasted_iota(jnp.int32, (n, n), 0) == lax.broadcasted_iota(jnp.int32, (n, n), 1)
    ).astype(F32)
    p = jnp.concatenate([eye + conjugacy.T, -step1.T], axis=1)
    second.send_z()
    basis[n:, LANES:] = v2
    ahead = dot_nn(p, basis[...])
    moved = dot_nn(step1.T, basis[:n, :])
    on_v1 = dot_nn(p, gram[:, n:])
    second.send_result()
    on_v2 = dot_nt(p, second.finish())
    curvature = dot_nt(jnp.concatenate([on_v1, on_v2], axis=1), p)
    step2 = eliminate(0.5 * (curvature + curvature.T), next_squares).T
    update = dot_nn(step2, ahead)
    w_ref[...] = moved[:, :LANES] + update[:, :LANES]
    r_ref[...] = (v0 - moved[:, LANES:]) - update[:, LANES:]
    for copy in sends:
        copy.wait_send()


def solution(mesh):
    R, T = mesh.shape["region"], mesh.shape["tile"]
    NY = 8 if R % 8 == 0 else 2
    NZ = R // NY

    def shards(innovations, obs_geometry, obs_error, tile_owner):
        n, m = innovations.shape
        reach = tile_owner.shape[1]
        S = 2 * reach - 1
        copies = 3 * 2 * (reach - 1) + 3 * (T - 1) + 2 * (2 * (T - 1) + NY - 1 + NZ - 1)
        h1, h2 = 2 * n // T, n // T

        def buffer(count, rows):
            return pltpu.VMEM((count, rows, LANES), F32)

        def sum_buffers(h):
            return [buffer(T, h), buffer(T, h), buffer(NY, h), buffer(NZ, h), buffer(T, h)]

        return pl.pallas_call(
            functools.partial(kernel, (R, T, NY, reach)),
            out_shape=[jax.ShapeDtypeStruct((n, m), F32)] * 2,
            in_specs=[pl.BlockSpec(memory_space=pltpu.VMEM)] * 4,
            out_specs=[pl.BlockSpec(memory_space=pltpu.VMEM)] * 2,
            scratch_shapes=[
                buffer(S, 8), buffer(T, 8),
                buffer(S, LANES), buffer(S, LANES), buffer(S, LANES),
                pltpu.VMEM((S, n, LANES), BF16), pltpu.VMEM((S, n, LANES), BF16),
                pltpu.VMEM((T, S, LANES, LANES), BF16),
                buffer(T, n), buffer(T, n), buffer(T - 1, n), buffer(T - 1, n),
                pltpu.VMEM((n, LANES), F32), pltpu.VMEM((n, LANES), F32), pltpu.VMEM((2 * n, 2 * LANES), F32),
                *sum_buffers(h1), *sum_buffers(h2),
                pltpu.SemaphoreType.DMA((copies,)), pltpu.SemaphoreType.DMA((copies,)),
            ],
            compiler_params=pltpu.CompilerParams(collective_id=0, has_side_effects=True),
        )(innovations, obs_geometry, obs_error.reshape(1, m), tile_owner)

    return jax.shard_map(
        shards,
        mesh=mesh,
        in_specs=(
            P(None, ("region", "tile")),
            P(None, ("region", "tile")),
            P(("region", "tile")),
            P("region", None),
        ),
        out_specs=(P(None, ("region", "tile")), P(None, ("region", "tile"))),
        check_vma=False,
    )
```

time: 750 us -> 91.9 us (0.12); the launches traced: 742 us -> 91.7 us
  blocking collectives: 350 us -> 0 us
  waiting for transfers between devices: 187 us -> 0 us
  starting transfers between devices: 100 us -> 0 us
  Pallas kernels: 0 us -> 89 us
  other arithmetic: 49.8 us -> 0 us
  between operations: 19.7 us -> 0.65 us
  local copies, waits for them, and re-layouts: 19.4 us -> 2 us
  matrix products: 15.5 us -> 0 us
    psum x3 -> x0, blocking collectives: 294 us -> none  [the longest x1 99.7 us: shards(): squares = lax.psum(gram_matrix(residual, residual), ('region', 'tile'))]
    ppermute x30 -> x0, waiting for transfers between devices: 101 us -> none  [from_behind(): return lax.ppermute(block, axis, route)]
    ppermute x30 -> x0, starting transfers between devices: 100 us -> none  [from_behind(): return lax.ppermute(block, axis, route)]
    pallas_call x0 -> x1, Pallas kernels: none -> 89 us  [shards(): pl.pallas_call(functools.partial(kernel, (R, T, NY, reach)), out_shape=[j...]
    reduce_scatter x2 -> x0, waiting for transfers between devices: 85.3 us -> none  [shards(): lax.psum_scatter(total_block, 'tile', scatter_dimension=1, tiled=True)]
    all_gather x3 -> x0, blocking collectives: 56.4 us -> none  [the longest x2 33.3 us: shards(): blocks = lax.all_gather(jnp.stack(pieces), 'tile', axis=2, tiled=True)]
    another operation x15 -> x0, other arithmetic: 36.2 us -> none  [the longest x9 19.6 us: gram_solve(): factor = jnp.linalg.cholesky(symmetric)]
    another operation x31 -> x0, local copies, waits for them, and re-layouts: 16.4 us -> none
  transfers between devices with their start and end apart: 32 -> 0, of which waited for: 18 -> 0; matrix products, arithmetic and copies ran while one was open for 5% -> 0% of each run, Pallas kernels for 0% -> 0%
where the time goes in v1:
time: 91.9 us; the launch traced here: 91.7 us
  Pallas kernels  89 us (97%)
  local copies, waits for them, and re-layouts  2 us (2%)
    pallas_call x1, Pallas kernels, shards(): pl.pallas_call(functools.partial(kernel, (R, T, NY, reach)), out_shape=[j...  89 us
    unnamed x4, local copies, waits for them, and re-layouts  2 us

profile of v1, /device:TPU:1, one launch (start us, length us, event | category | flops | bytes accessed | tf_op | source)
XLA Modules:
  0.0 91.7 jit_solution(3422652643937529034)
XLA Ops:
  0.6 89.0 %shard_map.59 = (f32[64,128]{1,0:T(8,128)}, f32[64,128]{1,0:T(8,128)}) custom-call(f32[64,128]{1,0:T(8,128)} %v0_ref.1, f32[3,128]{1,0:T(4,128)} %geo_ref.1, f32[1,128]{1,0:T(1,128)} %bitcast.1, s32[1,7]{1,0:T(1,128)} %own_ref.1), custom_call_target="tpu_custom_call" | custom-call | tf_op jit(solution)/shard_map/pallas_call | solution.py:295
  89.7 0.0 copy-start
  89.7 1.4 %copy.8 = f32[64,128]{1,0:T(8,128)} copy(f32[64,128]{1,0:T(8,128)} %get-tuple-element.4) | data formatting | bytes 65536
  91.1 0.0 copy-done
  91.1 0.6 copy.9
Async XLA Ops:
  89.7 1.4 %copy-start = (f32[64,128]{1,0:T(8,128)S(1)}, f32[64,128]{1,0:T(8,128)}, u32[]{:S(2)}) copy-start(f32[64,128]{1,0:T(8,128)} %get-tuple-element.5) | copy-start | bytes 98308

commit v2 on v1

--- a/solution.py
+++ b/solution.py
@@ -25,10 +25,30 @@
 def eliminate(matrix, target):
     n = matrix.shape[0]
     work = jnp.concatenate([matrix, target], axis=1)
+    work = work * (1.0 / work[0:1, 0:1])
     rows = lax.broadcasted_iota(jnp.int32, (n, 1), 0)
-    for k in range(n):
-        row = work[k : k + 1, :] * (1.0 / work[k : k + 1, k : k + 1])
-        work = jnp.where(rows == k, row, work - work[:, k : k + 1] * row)
+    for k in range(0, n, 4):
+        col = [jnp.broadcast_to(work[:, k + i : k + i + 1], work.shape) for i in range(4)]
+        row = [work[k + i : k + i + 1, :] for i in range(4)]
+
+        def at(i, j):
+            return col[j][k + i : k + i + 1, :]
+
+        a, b, c = at(0, 0), at(0, 1), at(1, 1)
+        e, f, g, h = at(0, 2), at(0, 3), at(1, 2), at(1, 3)
+        p, q, s = at(2, 2), at(2, 3), at(3, 3)
+        inverse = 1.0 / (a * c - b * b)
+        n0, n1 = (c * row[0] - b * row[1]) * inverse, (a * row[1] - b * row[0]) * inverse
+        e1, f1 = (c * e - b * g) * inverse, (c * f - b * h) * inverse
+        g1, h1 = (a * g - b * e) * inverse, (a * h - b * f) * inverse
+        p, q, s = p - (e * e1 + g * g1), q - (e * f1 + g * h1), s - (f * f1 + h * h1)
+        r2, r3 = row[2] - (e * n0 + g * n1), row[3] - (f * n0 + h * n1)
+        inverse = 1.0 / (p * s - q * q)
+        m2, m3 = (s * r2 - q * r3) * inverse, (p * r3 - q * r2) * inverse
+        m0, m1 = n0 - (e1 * m2 + f1 * m3), n1 - (g1 * m2 + h1 * m3)
+        work = work - (col[0] * m0 + col[1] * m1) - (col[2] * m2 + col[3] * m3)
+        for i, solved in enumerate((m0, m1, m2, m3)):
+            work = jnp.where(rows == k + i, solved, work)
     return work[:, n:]
 
 
@@ -62,7 +82,7 @@
 
 def kernel(
     cfg, v0_ref, geo_ref, err_ref, own_ref, w_ref, r_ref,
-    pb, hb, xb, yb, sb, ub0, ub1, cb, acc0, acc1, rs0, rs1, v1_ref, v2_ref, basis,
+    pb, hb, xb, yb, sb, ub0, ub1, cb, acc0, acc1, rs0, rs1, v1_ref, vt, basis,
     l1, t1, y1, z1, g1, l2, t2, y2, z2, g2, send_sems, recv_sems,
 ):
     R, T, NY, REACH = cfg
@@ -74,7 +94,12 @@
     t = lax.axis_index("tile")
     y = lax.rem(r, NY)
     z = lax.div(r, NY)
-    offsets = [d for k in range(1, REACH) for d in (k, -k)]
+    offsets = [d for k in sorted(range(1, REACH), key=lambda k: -min(k, NY - k)) for d in (k, -k)]
+    split = REACH // 2 + 1
+    far = [i for i, d in enumerate(offsets) if abs(d) >= split]
+    near = [i for i, d in enumerate(offsets) if abs(d) < split]
+    far_slots = list(range(0, mid - split + 1)) + list(range(mid + split, S))
+    near_slots = list(range(mid - split + 1, mid + split))
 
     def region(d):
         return (lax.rem(r + d + R, R), t)
@@ -106,9 +131,9 @@
     pb[mid, 2:3, :] = geo_ref[2:3, :]
     pb[mid, 3:4, :] = jnp.zeros((1, LANES), F32)
     pb[mid, 3:4, 0:REACH] = jnp.where(own_ref[0:1, :] >= 0, 1.0, 0.0)
-    pb[mid, 4:8, :] = jnp.zeros((4, LANES), F32)
     hb[0] = pb[mid]
     ub0[mid] = v0_ref[...].astype(BF16)
+    vt[0, :n] = v0_ref[...]
 
     pl.semaphore_wait(barrier, len(peers))
 
@@ -120,7 +145,9 @@
         sends.append(home_stage.copy(hb.at[0], hb.at[o], o - 1, along_tile(o)))
     for index, d in enumerate(offsets):
         sends.append(u0_stage.copy(ub0.at[mid], ub0.at[mid - d], index, region(d)))
-    for copy in sends:
+    begin_stage = stage(T - 1)
+    begin_copies = [begin_stage.copy(vt.at[0, :n], vt.at[o, :n], o - 1, along_tile(o)) for o in range(1, T)]
+    for copy in sends + begin_copies:
         copy.start()
     for copy in sends[: len(offsets) + T - 1]:
         copy.wait_recv()
@@ -143,35 +170,50 @@
 
     lax.fori_loop(0, S, build, 0)
 
-    def apply(ub, acc, rs, v_ref, out_ref):
+    def product(ub, acc, slots, add=False, copies=None):
+        whole = jnp.concatenate([ub[s] for s in slots], axis=1)
+        low, high = [s for s in slots if s < mid], [s for s in slots if s >= mid]
+        runs = [low, high] if low and high and low[-1] + 1 != high[0] else [slots]
+
+        def chunk(step, carry):
+            o = lax.rem(step + 1, T)
+            tiles = [cb[o, run[0] : run[-1] + 1].reshape(len(run) * LANES, LANES) for run in runs]
+            tiles = tiles[0] if len(tiles) == 1 else jnp.concatenate(tiles, axis=0)
+            value = jnp.dot(whole, tiles, preferred_element_type=F32)
+            acc[o] = acc[o] + value if add else value
+            if copies is not None:
+
+                @pl.when(step >= 1)
+                def _():
+                    copies(step).start()
+
+            return carry
+
+        lax.fori_loop(0, T, chunk, 0)
+
+    def scatter(acc, rs):
         found = stage(T - 1)
-        whole = jnp.concatenate([ub[s] for s in range(S)], axis=1)
-
-        def out_copy(o):
+
+        def copies(o):
             return found.copy(acc.at[o], rs.at[o - 1], o - 1, (r, lax.rem(t - o + T, T)))
 
-        def product(step, carry):
-            o = lax.rem(step + 1, T)
-            acc[o] = jnp.dot(whole, cb[o].reshape(S * LANES, LANES), preferred_element_type=F32)
-
-            @pl.when(step >= 1)
-            def _():
-                out_copy(step).start()
-
-            return carry
-
-        lax.fori_loop(0, T, product, 0)
-        total = err_ref[...] * v_ref[...] + acc[0]
+        return copies
+
+    def gathered(acc, rs, copies):
+        total = acc[0]
         for o in range(1, T):
-            copy = out_copy(o)
+            copy = copies(o)
             copy.wait_recv()
             total = total + rs[o - 1]
             sends.append(copy)
-        out_ref[...] = total
+        return total
 
     for copy in sends[len(offsets) + T - 1 :]:
         copy.wait_recv()
-    apply(ub0, acc0, rs0, v0_ref, v1_ref)
+    sends.extend(begin_copies)
+    scatter0 = scatter(acc0, rs0)
+    product(ub0, acc0, list(range(S)), copies=scatter0)
+    v1_ref[...] = err_ref[...] * v0_ref[...] + gathered(acc0, rs0, scatter0)
 
     ub1[mid] = v1_ref[...].astype(BF16)
     u1_stage = stage(len(offsets))
@@ -231,39 +273,57 @@
 
     for copy in u1_copies:
         copy.start()
-        sends.append(copy)
-    basis[:n, :LANES] = v0_ref[...]
-    basis[n:, :LANES] = v1_ref[...]
-    basis[:n, LANES:] = v1_ref[...]
-    both = basis[:, :LANES]
+    sends.extend(u1_copies)
+    vt[0, n:] = v1_ref[...]
+    both = vt[0]
     l1[...] = dot_nt(both, both).reshape(l1.shape)
     first.send_tile()
+    basis_stage = stage(T - 1)
+    basis_copies = [basis_stage.copy(vt.at[0, n:], vt.at[o, n:], o - 1, along_tile(o)) for o in range(1, T)]
+    for copy in basis_copies:
+        copy.start()
+    sends.extend(basis_copies)
     first.send_y()
-    for copy in u1_copies:
+    for index in far:
+        u1_copies[index].wait_recv()
+    product(ub1, acc1, far_slots)
+    first.send_z()
+    for index in near:
+        u1_copies[index].wait_recv()
+    product(ub1, acc1, near_slots, add=True)
+    acc1[0] = acc1[0] + err_ref[...] * v1_ref[...]
+
+    for copy in begin_copies + basis_copies:
         copy.wait_recv()
-    apply(ub1, acc1, rs1, v1_ref, v2_ref)
-    l2[...] = dot_nt(v2_ref[...], both).reshape(l2.shape)
+    part = jnp.concatenate([acc1[o] for o in range(T)], axis=1)
+    whole = jnp.concatenate([vt[o] for o in range(T)], axis=1)
+    l2[...] = dot_nt(part, whole).reshape(l2.shape)
     second.send_tile()
-    first.send_z()
+    scatter1 = scatter(acc1, rs1)
+    for o in range(1, T):
+        scatter1(o).start()
+    first.send_result()
     second.send_y()
-    first.send_result()
-
-    v0, v1, v2 = v0_ref[...], v1_ref[...], v2_ref[...]
+
     gram = first.finish()
     g00, g01, g10, g11 = gram[:n, :n], gram[:n, n:], gram[n:, :n], gram[n:, n:]
     step1 = eliminate(0.5 * (g01 + g01.T), g00)
     next_squares = (g00 - dot_nn(g01, step1)) - dot_nn(step1.T, g10 - dot_nn(g11, step1))
+    second.send_z()
     conjugacy = eliminate(0.5 * (g00 + g00.T), next_squares)
     eye = (
         lax.broadcasted_iota(jnp.int32, (n, n), 0) == lax.broadcasted_iota(jnp.int32, (n, n), 1)
     ).astype(F32)
     p = jnp.concatenate([eye + conjugacy.T, -step1.T], axis=1)
-    second.send_z()
-    basis[n:, LANES:] = v2
+    on_v1 = dot_nn(p, gram[:, n:])
+    second.send_result()
+    v0, v1 = v0_ref[...], v1_ref[...]
+    basis[:n, :LANES] = v0
+    basis[n:, :LANES] = v1
+    basis[:n, LANES:] = v1
+    basis[n:, LANES:] = gathered(acc1, rs1, scatter1)
     ahead = dot_nn(p, basis[...])
     moved = dot_nn(step1.T, basis[:n, :])
-    on_v1 = dot_nn(p, gram[:, n:])
-    second.send_result()
     on_v2 = dot_nt(p, second.finish())
     curvature = dot_nt(jnp.concatenate([on_v1, on_v2], axis=1), p)
     step2 = eliminate(0.5 * (curvature + curvature.T), next_squares).T
@@ -283,7 +343,7 @@
         n, m = innovations.shape
         reach = tile_owner.shape[1]
         S = 2 * reach - 1
-        copies = 3 * 2 * (reach - 1) + 3 * (T - 1) + 2 * (2 * (T - 1) + NY - 1 + NZ - 1)
+        copies = 3 * 2 * (reach - 1) + 5 * (T - 1) + 2 * (2 * (T - 1) + NY - 1 + NZ - 1)
         h1, h2 = 2 * n // T, n // T
 
         def buffer(count, rows):
@@ -298,12 +358,12 @@
             in_specs=[pl.BlockSpec(memory_space=pltpu.VMEM)] * 4,
             out_specs=[pl.BlockSpec(memory_space=pltpu.VMEM)] * 2,
             scratch_shapes=[
-                buffer(S, 8), buffer(T, 8),
+                buffer(S, 4), buffer(T, 4),
                 buffer(S, LANES), buffer(S, LANES), buffer(S, LANES),
                 pltpu.VMEM((S, n, LANES), BF16), pltpu.VMEM((S, n, LANES), BF16),
                 pltpu.VMEM((T, S, LANES, LANES), BF16),
                 buffer(T, n), buffer(T, n), buffer(T - 1, n), buffer(T - 1, n),
-                pltpu.VMEM((n, LANES), F32), pltpu.VMEM((n, LANES), F32), pltpu.VMEM((2 * n, 2 * LANES), F32),
+                pltpu.VMEM((n, LANES), F32), buffer(T, 2 * n), pltpu.VMEM((2 * n, 2 * LANES), F32),
                 *sum_buffers(h1), *sum_buffers(h2),
                 pltpu.SemaphoreType.DMA((copies,)), pltpu.SemaphoreType.DMA((copies,)),
             ],

time: 91.9 us -> 77.9 us (0.85)
  Pallas kernels: 89 us -> 75 us
    pallas_call x1, Pallas kernels: 89 us -> 75 us  [shards(): pl.pallas_call(functools.partial(kernel, (R, T, NY, reach)), out_shape=[j...]
where the time goes in v2:
time: 77.9 us; the launch traced here: 77.6 us
  Pallas kernels  75 us (96%)
  local copies, waits for them, and re-layouts  2 us (3%)
    pallas_call x1, Pallas kernels, shards(): pl.pallas_call(functools.partial(kernel, (R, T, NY, reach)), out_shape=[j...  75 us
    unnamed x4, local copies, waits for them, and re-layouts  2 us

profile of v2, /device:TPU:1, one launch (start us, length us, event | category | flops | bytes accessed | tf_op | source)
XLA Modules:
  0.0 77.6 jit_solution(14033740978555203063)
XLA Ops:
  0.6 75.0 %shard_map.59 = (f32[64,128]{1,0:T(8,128)}, f32[64,128]{1,0:T(8,128)}) custom-call(f32[64,128]{1,0:T(8,128)} %v0_ref.1, f32[3,128]{1,0:T(4,128)} %geo_ref.1, f32[1,128]{1,0:T(1,128)} %bitcast.1, s32[1,7]{1,0:T(1,128)} %own_ref.1), custom_call_target="tpu_custom_call" | custom-call | tf_op jit(solution)/shard_map/pallas_call | solution.py:355
  75.6 0.0 copy-start
  75.7 1.4 %copy.8 = f32[64,128]{1,0:T(8,128)} copy(f32[64,128]{1,0:T(8,128)} %get-tuple-element.4) | data formatting | bytes 65536
  77.0 0.0 copy-done
  77.0 0.6 copy.9
Async XLA Ops:
  75.6 1.4 %copy-start = (f32[64,128]{1,0:T(8,128)S(1)}, f32[64,128]{1,0:T(8,128)}, u32[]{:S(2)}) copy-start(f32[64,128]{1,0:T(8,128)} %get-tuple-element.5) | copy-start | bytes 98308

commit v3 on v2

v3 whole, which is shorter than its diff:
```python
import functools

import jax
import jax.numpy as jnp
from jax import lax
from jax.experimental import pallas as pl
from jax.experimental.pallas import tpu as pltpu
from jax.sharding import PartitionSpec as P

MESH = pl.DeviceIdType.MESH
F32 = jnp.float32
BF16 = jnp.bfloat16
HI = lax.Precision.HIGHEST
LANES = 128
RELAY = {4: 2, -4: -2, 3: 2, -3: -2, 5: 6, -5: -6}


def dot_nn(a, b):
    return lax.dot_general(a, b, (((1,), (0,)), ((), ())), precision=HI, preferred_element_type=F32)


def dot_nt(a, b):
    return lax.dot_general(a, b, (((1,), (1,)), ((), ())), precision=HI, preferred_element_type=F32)


def system(matrix, target):
    work = jnp.concatenate([0.5 * (matrix + matrix.T), target], axis=1)
    return work * (1.0 / work[0:1, 0:1])


def pivots(work, start, stop):
    n = work.shape[0]
    rows = lax.broadcasted_iota(jnp.int32, (n, 1), 0)
    for k in range(start, stop, 4):
        col = [jnp.broadcast_to(work[:, k + i : k + i + 1], work.shape) for i in range(4)]
        row = [work[k + i : k + i + 1, :] for i in range(4)]

        def at(i, j):
            return col[j][k + i : k + i + 1, :]

        a, b, c = at(0, 0), at(0, 1), at(1, 1)
        e, f, g, h = at(0, 2), at(0, 3), at(1, 2), at(1, 3)
        p, q, s = at(2, 2), at(2, 3), at(3, 3)
        inverse = 1.0 / (a * c - b * b)
        n0, n1 = (c * row[0] - b * row[1]) * inverse, (a * row[1] - b * row[0]) * inverse
        e1, f1 = (c * e - b * g) * inverse, (c * f - b * h) * inverse
        g1, h1 = (a * g - b * e) * inverse, (a * h - b * f) * inverse
        p, q, s = p - (e * e1 + g * g1), q - (e * f1 + g * h1), s - (f * f1 + h * h1)
        r2, r3 = row[2] - (e * n0 + g * n1), row[3] - (f * n0 + h * n1)
        inverse = 1.0 / (p * s - q * q)
        m2, m3 = (s * r2 - q * r3) * inverse, (p * r3 - q * r2) * inverse
        m0, m1 = n0 - (e1 * m2 + f1 * m3), n1 - (g1 * m2 + h1 * m3)
        work = work - (col[0] * m0 + col[1] * m1) - (col[2] * m2 + col[3] * m3)
        for i, solved in enumerate((m0, m1, m2, m3)):
            work = jnp.where(rows == k + i, solved, work)
    return work


def tile_block(x_far, y_far, s_far, x_home, y_home, s_home):
    dx = x_far - x_home
    dy = y_far - y_home
    square = jnp.maximum(dx * dx + dy * dy, 1e-30)
    inverse = lax.rsqrt(square)
    z = square * inverse
    near = ((((-0.25 * z + 0.5) * z + 0.625) * z) - 5.0 / 3.0) * square + 1.0
    rest = jnp.maximum(2.0 - z, 0.0)
    rest2 = rest * rest
    far = rest2 * rest2 * ((z * (1.0 / 12.0) + 1.0 / 6.0) - inverse * (1.0 / 24.0))
    return (s_far * s_home) * jnp.where(z <= 1.0, near, far)


class Exchange:
    def __init__(self, send_sems, recv_sems, base):
        self.send_sems, self.recv_sems, self.base = send_sems, recv_sems, base

    def copy(self, src, dst, index, device):
        return pltpu.make_async_remote_copy(
            src_ref=src,
            dst_ref=dst,
            send_sem=self.send_sems.at[self.base + index],
            recv_sem=self.recv_sems.at[self.base + index],
            device_id=device,
            device_id_type=MESH,
        )


def kernel(
    cfg, v0_ref, geo_ref, err_ref, own_ref, w_ref, r_ref,
    pb, hb, xb, yb, sb, ub0, ub1, cb, acc0, acc1, rs0, rs1, v1_ref, vt, basis,
    l0, t0, y0, z0, g0, l1, t1, y1, z1, g1, l2, t2, y2, z2, g2, send_sems, recv_sems,
):
    R, T, NY, REACH = cfg
    NZ = R // NY
    S = 2 * REACH - 1
    n = v0_ref.shape[0]
    mid = REACH - 1
    r = lax.axis_index("region")
    t = lax.axis_index("tile")
    y = lax.rem(r, NY)
    z = lax.div(r, NY)
    offsets = [d for k in sorted(range(1, REACH), key=lambda k: -min(k, NY - k)) for d in (k, -k)]
    route = {d: via for d, via in RELAY.items() if d in offsets and via in offsets}
    early = [mid] + [mid - d for d in offsets if d not in route]
    late = [mid - d for d in offsets if d in route]
    close = min(2, REACH - 1)

    def region(d):
        return (lax.rem(r + d + R, R), t)

    def along_tile(o):
        return (r, lax.rem(t + o, T))

    def along_y(o):
        return (z * NY + lax.rem(y + o, NY), t)

    def along_z(o):
        return (lax.rem(z + o, NZ) * NY + y, t)

    def farthest_first(count):
        return sorted(range(1, count), key=lambda o: -min(o, count - o))

    peers = [region(d) for d in offsets] + [along_tile(o) for o in range(1, T)]
    peers += [along_y(o) for o in range(1, NY)] + [along_z(o) for o in range(1, NZ)]

    barrier = pltpu.get_barrier_semaphore()
    for peer in peers:
        pl.semaphore_signal(barrier, inc=1, device_id=peer, device_id_type=MESH)

    base = [0]

    def stage(count):
        made = Exchange(send_sems, recv_sems, base[0])
        base[0] += count
        return made

    pb[mid, 0:2, :] = geo_ref[0:2, :] * 2.0
    pb[mid, 2:3, :] = geo_ref[2:3, :]
    pb[mid, 3:4, :] = jnp.zeros((1, LANES), F32)
    pb[mid, 3:4, 0:REACH] = jnp.where(own_ref[0:1, :] >= 0, 1.0, 0.0)
    hb[0] = pb[mid]
    ub0[mid] = v0_ref[...].astype(BF16)
    vt[0, :n] = v0_ref[...]

    start_gram = dot_nt(v0_ref[...], v0_ref[...])
    l0[...] = jnp.concatenate([start_gram, start_gram], axis=1).reshape(l0.shape)

    pl.semaphore_wait(barrier, len(peers))

    class Sum:
        def __init__(self, local, tile_part, y_part, z_part, result):
            self.local, self.parts, self.result = local, (tile_part, y_part, z_part), result
            self.stages = [stage(T - 1), stage(NY - 1), stage(NZ - 1), stage(T - 1)]
            self.pending = []

        def start(self, copies):
            for copy in copies:
                copy.start()
            self.pending = copies
            sends.extend(copies)

        def wait(self):
            for copy in self.pending:
                copy.wait_recv()

        def send_tile(self):
            self.parts[0][t] = self.local[t]
            self.start([
                self.stages[0].copy(self.local.at[lax.rem(t + o, T)], self.parts[0].at[t], o - 1, along_tile(o))
                for o in farthest_first(T)
            ])

        def total(self, part, count):
            self.wait()
            value = part[0]
            for i in range(1, count):
                value = value + part[i]
            return value

        def send_y(self):
            self.parts[1][y] = self.total(self.parts[0], T)
            part = self.parts[1].at[y]
            self.start([self.stages[1].copy(part, part, o - 1, along_y(o)) for o in farthest_first(NY)])

        def send_z(self):
            self.parts[2][z] = self.total(self.parts[1], NY)
            part = self.parts[2].at[z]
            self.start([self.stages[2].copy(part, part, o - 1, along_z(o)) for o in farthest_first(NZ)])

        def send_result(self):
            self.result[t] = self.total(self.parts[2], NZ)
            part = self.result.at[t]
            self.start([self.stages[3].copy(part, part, o - 1, along_tile(o)) for o in farthest_first(T)])

        def finish(self):
            self.wait()
            return self.result[...].reshape(-1, LANES)

    start = Sum(l0, t0, y0, z0, g0)
    first = Sum(l1, t1, y1, z1, g1)
    second = Sum(l2, t2, y2, z2, g2)

    geo_stage, home_stage, u0_stage, begin_stage = stage(len(offsets)), stage(T - 1), stage(len(offsets)), stage(T - 1)
    geo_copies = {d: geo_stage.copy(pb.at[mid], pb.at[mid - d], i, region(d)) for i, d in enumerate(offsets)}
    home_copies = [home_stage.copy(hb.at[0], hb.at[o], o - 1, along_tile(o)) for o in farthest_first(T)]
    u0_copies = [u0_stage.copy(ub0.at[mid], ub0.at[mid - d], i, region(d)) for i, d in enumerate(offsets)]
    begin_copies = [begin_stage.copy(vt.at[0, :n], vt.at[o, :n], o - 1, along_tile(o)) for o in farthest_first(T)]
    sends = [*geo_copies.values(), *home_copies, *u0_copies, *begin_copies]
    for copy in [*geo_copies.values(), *home_copies]:
        copy.start()
    start.send_tile()
    for copy in u0_copies + begin_copies:
        copy.start()

    def spread(s):
        block = pb[s]
        d = s - mid
        listed = pb[mid if d >= 0 else s, 3:4, abs(d) : abs(d) + 1]
        columns = block.T
        xb[s] = jnp.broadcast_to(columns[:, 0:1], (LANES, LANES))
        yb[s] = jnp.broadcast_to(columns[:, 1:2], (LANES, LANES))
        sb[s] = jnp.broadcast_to(columns[:, 2:3] * listed, (LANES, LANES))

    def build(step, carry):
        for o in range(T):
            home = hb[o]
            block = tile_block(xb[step], yb[step], sb[step], home[0:1, :], home[1:2, :], home[2:3, :])
            cb[o, step] = block.astype(BF16)
        return carry

    spread(mid)
    for copy in home_copies:
        copy.wait_recv()
    for d in offsets:
        if abs(d) <= close:
            geo_copies[d].wait_recv()
            spread(mid - d)
    lax.fori_loop(mid - close, mid + close + 1, build, 0)
    for d in offsets:
        if abs(d) > close:
            geo_copies[d].wait_recv()
            spread(mid - d)
    start.send_y()
    lax.fori_loop(0, mid - close, build, 0)
    lax.fori_loop(mid + close + 1, S, build, 0)

    def product(ub, acc, slots, add=False, copies=None):
        slots = sorted(slots)
        whole = jnp.concatenate([ub[s] for s in slots], axis=1)
        runs = []
        for s in slots:
            if runs and runs[-1][1] == s:
                runs[-1][1] = s + 1
            else:
                runs.append([s, s + 1])

        def order(step):
            half = lax.div(step + 1, 2)
            return T // 2 + half - 2 * half * lax.rem(step, 2)

        def chunk(step, carry):
            o = order(step)
            tiles = [cb[o, a:b].reshape((b - a) * LANES, LANES) for a, b in runs]
            tiles = tiles[0] if len(tiles) == 1 else jnp.concatenate(tiles, axis=0)
            value = jnp.dot(whole, tiles, preferred_element_type=F32)
            acc[o] = acc[o] + value if add else value
            if copies is not None:

                @pl.when(step >= 1)
                def _():
                    copies(order(step - 1)).start()

            return carry

        lax.fori_loop(0, T, chunk, 0)

    def scatter(acc, rs):
        found = stage(T - 1)

        def copies(o):
            return found.copy(acc.at[o], rs.at[o - 1], o - 1, (r, lax.rem(t - o + T, T)))

        return copies

    def gathered(acc, rs, copies):
        total = acc[0]
        for o in range(1, T):
            copy = copies(o)
            copy.wait_recv()
            total = total + rs[o - 1]
            sends.append(copy)
        return total

    start.send_z()
    for copy in u0_copies:
        copy.wait_recv()
    scatter0 = scatter(acc0, rs0)
    product(ub0, acc0, list(range(S)), copies=scatter0)
    start.send_result()
    v1_ref[...] = err_ref[...] * v0_ref[...] + gathered(acc0, rs0, scatter0)

    ub1[mid] = v1_ref[...].astype(BF16)
    u1_stage = stage(len(offsets))
    u1_copies = {}
    for i, d in enumerate(offsets):
        via = route.get(d, 0)
        u1_copies[d] = u1_stage.copy(ub1.at[mid - via], ub1.at[mid - d], i, region(d - via))

    for d in offsets:
        if d not in route:
            u1_copies[d].start()
    vt[0, n:] = v1_ref[...]
    both = vt[0]
    l1[...] = dot_nt(v1_ref[...], both).reshape(l1.shape)
    first.send_tile()
    eye = (
        lax.broadcasted_iota(jnp.int32, (n, n), 0) == lax.broadcasted_iota(jnp.int32, (n, n), 1)
    ).astype(F32)
    for d in sorted(set(route.values()), key=abs):
        u1_copies[d].wait_recv()
        for beyond in offsets:
            if route.get(beyond) == d:
                u1_copies[beyond].start()
    sends.extend(u1_copies.values())
    first.send_y()
    basis_stage = stage(T - 1)
    basis_copies = [basis_stage.copy(vt.at[0, n:], vt.at[o, n:], o - 1, along_tile(o)) for o in farthest_first(T)]
    for copy in basis_copies:
        copy.start()
    sends.extend(basis_copies)
    for d in offsets:
        if d not in route and d not in route.values():
            u1_copies[d].wait_recv()
    product(ub1, acc1, early)
    for d in offsets:
        if d in route:
            u1_copies[d].wait_recv()
    if late:
        product(ub1, acc1, late, add=True)
    first.send_z()
    acc1[0] = acc1[0] + err_ref[...] * v1_ref[...]

    for copy in begin_copies + basis_copies:
        copy.wait_recv()
    part = jnp.concatenate([acc1[o] for o in range(T)], axis=1)
    whole = jnp.concatenate([vt[o] for o in range(T)], axis=1)
    l2[...] = dot_nt(part, whole).reshape(l2.shape)
    second.send_tile()
    g00 = start.finish()[:, :n]
    inverse = pivots(system(g00, eye * g00[0:1, 0:1]), 0, n)[:, n:] * (1.0 / g00[0:1, 0:1])
    second.send_y()
    first.send_result()

    gram = first.finish()
    g10, g11 = gram[:, :n], gram[:, n:]
    g01 = g10.T
    scatter1 = scatter(acc1, rs1)
    for o in farthest_first(T):
        scatter1(o).start()
    second.send_z()
    step1 = pivots(system(g01, g00), 0, n)[:, n:]
    next_squares = (g00 - dot_nn(g01, step1)) - dot_nn(step1.T, g10 - dot_nn(g11, step1))
    conjugacy = dot_nn(inverse, next_squares)
    p = jnp.concatenate([eye + conjugacy.T, -step1.T], axis=1)
    second.send_result()
    on_v1 = dot_nn(p, jnp.concatenate([g01, g11], axis=0))
    v0, v1 = v0_ref[...], v1_ref[...]
    basis[:n, :LANES] = v0
    basis[n:, :LANES] = v1
    basis[:n, LANES:] = v1
    basis[n:, LANES:] = gathered(acc1, rs1, scatter1)
    ahead = dot_nn(p, basis[...])
    moved = dot_nn(step1.T, basis[:n, :])
    on_v2 = dot_nt(p, second.finish())
    curvature = dot_nt(jnp.concatenate([on_v1, on_v2], axis=1), p)
    step2 = pivots(system(curvature, next_squares), 0, n)[:, n:].T
    update = dot_nn(step2, ahead)
    w_ref[...] = moved[:, :LANES] + update[:, :LANES]
    r_ref[...] = (v0 - moved[:, LANES:]) - update[:, LANES:]
    for copy in sends:
        copy.wait_send()


def solution(mesh):
    R, T = mesh.shape["region"], mesh.shape["tile"]
    NY = 8 if R % 8 == 0 else 2
    NZ = R // NY

    def shards(innovations, obs_geometry, obs_error, tile_owner):
        n, m = innovations.shape
        reach = tile_owner.shape[1]
        S = 2 * reach - 1
        copies = 3 * 2 * (reach - 1) + 5 * (T - 1) + 3 * (2 * (T - 1) + NY - 1 + NZ - 1)

        def buffer(count, rows):
            return pltpu.VMEM((count, rows, LANES), F32)

        def sum_buffers(h):
            return [buffer(T, h), buffer(T, h), buffer(NY, h), buffer(NZ, h), buffer(T, h)]

        return pl.pallas_call(
            functools.partial(kernel, (R, T, NY, reach)),
            out_shape=[pltpu.VMEM((n, m), F32)] * 2,
            in_specs=[pl.BlockSpec(memory_space=pltpu.VMEM)] * 4,
            out_specs=[pl.BlockSpec(memory_space=pltpu.VMEM)] * 2,
            scratch_shapes=[
                buffer(S, 4), buffer(T, 4),
                buffer(S, LANES), buffer(S, LANES), buffer(S, LANES),
                pltpu.VMEM((S, n, LANES), BF16), pltpu.VMEM((S, n, LANES), BF16),
                pltpu.VMEM((T, S, LANES, LANES), BF16),
                buffer(T, n), buffer(T, n), buffer(T - 1, n), buffer(T - 1, n),
                pltpu.VMEM((n, LANES), F32), buffer(T, 2 * n), pltpu.VMEM((2 * n, 2 * LANES), F32),
                *sum_buffers(n // T), *sum_buffers(n // T), *sum_buffers(n // T),
                pltpu.SemaphoreType.DMA((copies,)), pltpu.SemaphoreType.DMA((copies,)),
            ],
            compiler_params=pltpu.CompilerParams(collective_id=0, has_side_effects=True),
        )(innovations, obs_geometry, obs_error.reshape(1, m), tile_owner)

    return jax.shard_map(
        shards,
        mesh=mesh,
        in_specs=(
            P(None, ("region", "tile")),
            P(None, ("region", "tile")),
            P(("region", "tile")),
            P("region", None),
        ),
        out_specs=(P(None, ("region", "tile")), P(None, ("region", "tile"))),
        check_vma=False,
    )
```

time: 77.9 us -> 75.1 us (0.964)
  Pallas kernels: 75 us -> 73 us
    pallas_call x1, Pallas kernels: 75 us -> 73 us  [shards(): pl.pallas_call(functools.partial(kernel, (R, T, NY, reach)), out_shape=[p...]
    unnamed x4 -> x2, local copies, waits for them, and re-layouts: 2 us -> 1.23 us
where the time goes in v3:
time: 75.1 us; the launch traced here: 74.9 us
  Pallas kernels  73 us (97%)
  local copies, waits for them, and re-layouts  1.23 us (2%)
    pallas_call x1, Pallas kernels, shards(): pl.pallas_call(functools.partial(kernel, (R, T, NY, reach)), out_shape=[p...  73 us

profile of v3, /device:TPU:1, one launch (start us, length us, event | category | flops | bytes accessed | tf_op | source)
XLA Modules:
  0.0 74.9 jit_solution(13356080655054817194)
XLA Ops:
  0.6 73.0 %shard_map.59 = (f32[64,128]{1,0:T(8,128)S(1)}, f32[64,128]{1,0:T(8,128)S(1)}) custom-call(f32[64,128]{1,0:T(8,128)} %v0_ref.1, f32[3,128]{1,0:T(4,128)} %geo_ref.1, f32[1,128]{1,0:T(1,128)} %bitcast.1, s32[1,7]{1,0:T(1,128)} %own_ref.1), custom_call_target="tpu_custom_call" | custom-call | tf_op jit(solution)/shard_map/pallas_call | solution.py:400
  73.6 0.6 copy.8
  74.3 0.6 copy.9

commit v4 on v3

--- a/solution.py
+++ b/solution.py
@@ -85,11 +85,18 @@
 
 
 def kernel(
-    cfg, v0_ref, geo_ref, err_ref, own_ref, w_ref, r_ref,
+    cfg, v0_in, geo_in, err_in, own_in, w_ref, r_ref,
+    v0_ref, geo_ref, err_ref, own_ref, in_sems,
     pb, hb, xb, yb, sb, ub0, ub1, cb, acc0, acc1, rs0, rs1, v1_ref, vt, basis,
     l0, t0, y0, z0, g0, l1, t1, y1, z1, g1, l2, t2, y2, z2, g2, send_sems, recv_sems,
 ):
     R, T, NY, REACH = cfg
+    loads = [
+        pltpu.make_async_copy(src, dst, in_sems.at[i])
+        for i, (src, dst) in enumerate([(geo_in, geo_ref), (own_in, own_ref), (v0_in, v0_ref), (err_in, err_ref)])
+    ]
+    for copy in loads:
+        copy.start()
     NZ = R // NY
     S = 2 * REACH - 1
     n = v0_ref.shape[0]
@@ -126,6 +133,8 @@
     for peer in peers:
         pl.semaphore_signal(barrier, inc=1, device_id=peer, device_id_type=MESH)
 
+    for copy in loads:
+        copy.wait()
     base = [0]
 
     def stage(count):
@@ -305,7 +314,7 @@
         via = route.get(d, 0)
         u1_copies[d] = u1_stage.copy(ub1.at[mid - via], ub1.at[mid - d], i, region(d - via))
 
-    for d in offsets:
+    for d in sorted(offsets, key=lambda d: (d not in route.values(), abs(d))):
         if d not in route:
             u1_copies[d].start()
     vt[0, n:] = v1_ref[...]
@@ -400,9 +409,11 @@
         return pl.pallas_call(
             functools.partial(kernel, (R, T, NY, reach)),
             out_shape=[pltpu.VMEM((n, m), F32)] * 2,
-            in_specs=[pl.BlockSpec(memory_space=pltpu.VMEM)] * 4,
+            in_specs=[pl.BlockSpec(memory_space=pl.ANY)] * 4,
             out_specs=[pl.BlockSpec(memory_space=pltpu.VMEM)] * 2,
             scratch_shapes=[
+                pltpu.VMEM((n, m), F32), pltpu.VMEM((3, m), F32), pltpu.VMEM((1, m), F32),
+                pltpu.VMEM((1, reach), jnp.int32), pltpu.SemaphoreType.DMA((4,)),
                 buffer(S, 4), buffer(T, 4),
                 buffer(S, LANES), buffer(S, LANES), buffer(S, LANES),
                 pltpu.VMEM((S, n, LANES), BF16), pltpu.VMEM((S, n, LANES), BF16),

time: 75.1 us -> 74.2 us (0.988)
  Pallas kernels: 73 us -> 72.2 us
    pallas_call x1, Pallas kernels: 73 us -> 72.2 us  [shards(): pl.pallas_call(functools.partial(kernel, (R, T, NY, reach)), out_shape=[p...]
where the time goes in v4:
time: 74.2 us; the launch traced here: 74 us
  Pallas kernels  72.2 us (97%)
  local copies, waits for them, and re-layouts  1.23 us (2%)
    pallas_call x1, Pallas kernels, shards(): pl.pallas_call(functools.partial(kernel, (R, T, NY, reach)), out_shape=[p...  72.2 us

profile of v4, /device:TPU:1, one launch (start us, length us, event | category | flops | bytes accessed | tf_op | source)
XLA Modules:
  0.0 74.0 jit_solution(2986995070022174443)
XLA Ops:
  0.6 72.2 %shard_map.59 = (f32[64,128]{1,0:T(8,128)S(1)}, f32[64,128]{1,0:T(8,128)S(1)}) custom-call(f32[64,128]{1,0:T(8,128)} %v0_in.1, f32[3,128]{1,0:T(4,128)} %geo_in.1, f32[1,128]{1,0:T(1,128)} %bitcast.1, s32[1,7]{1,0:T(1,128)} %own_in.1), custom_call_target="tpu_custom_call" | custom-call | tf_op jit(solution)/shard_map/pallas_call | solution.py:409
  72.8 0.6 copy.8
  73.4 0.6 copy.9

commit v5 on v4

--- a/solution.py
+++ b/solution.py
@@ -233,7 +233,7 @@
         for o in range(T):
             home = hb[o]
             block = tile_block(xb[step], yb[step], sb[step], home[0:1, :], home[1:2, :], home[2:3, :])
-            cb[o, step] = block.astype(BF16)
+            cb[o // 2, step, :, o % 2 * LANES : (o % 2 + 1) * LANES] = block.astype(BF16)
         return carry
 
     spread(mid)
@@ -264,23 +264,28 @@
 
         def order(step):
             half = lax.div(step + 1, 2)
-            return T // 2 + half - 2 * half * lax.rem(step, 2)
+            return T // 4 + half - 2 * half * lax.rem(step, 2)
 
         def chunk(step, carry):
-            o = order(step)
-            tiles = [cb[o, a:b].reshape((b - a) * LANES, LANES) for a, b in runs]
+            pair = order(step)
+            tiles = [cb[pair, a:b].reshape((b - a) * LANES, 2 * LANES) for a, b in runs]
             tiles = tiles[0] if len(tiles) == 1 else jnp.concatenate(tiles, axis=0)
             value = jnp.dot(whole, tiles, preferred_element_type=F32)
-            acc[o] = acc[o] + value if add else value
+            for i in range(2):
+                o, half = 2 * pair + i, value[:, i * LANES : (i + 1) * LANES]
+                acc[o] = acc[o] + half if add else half
             if copies is not None:
 
                 @pl.when(step >= 1)
                 def _():
-                    copies(order(step - 1)).start()
+                    for i in range(2):
+                        copies(2 * order(step - 1) + i).start()
 
             return carry
 
-        lax.fori_loop(0, T, chunk, 0)
+        lax.fori_loop(0, T // 2, chunk, 0)
+        if copies is not None:
+            copies(1).start()
 
     def scatter(acc, rs):
         found = stage(T - 1)
@@ -417,7 +422,7 @@
                 buffer(S, 4), buffer(T, 4),
                 buffer(S, LANES), buffer(S, LANES), buffer(S, LANES),
                 pltpu.VMEM((S, n, LANES), BF16), pltpu.VMEM((S, n, LANES), BF16),
-                pltpu.VMEM((T, S, LANES, LANES), BF16),
+                pltpu.VMEM((T // 2, S, LANES, 2 * LANES), BF16),
                 buffer(T, n), buffer(T, n), buffer(T - 1, n), buffer(T - 1, n),
                 pltpu.VMEM((n, LANES), F32), buffer(T, 2 * n), pltpu.VMEM((2 * n, 2 * LANES), F32),
                 *sum_buffers(n // T), *sum_buffers(n // T), *sum_buffers(n // T),

time: 74.2 us -> 73.9 us (level)
  no operation moved by 1% of the time
where the time goes in v5:
time: 73.9 us; the launch traced here: 73.7 us
  Pallas kernels  71.9 us (97%)
  local copies, waits for them, and re-layouts  1.23 us (2%)
    pallas_call x1, Pallas kernels, shards(): pl.pallas_call(functools.partial(kernel, (R, T, NY, reach)), out_shape=[p...  71.9 us

profile of v5, /device:TPU:1, one launch (start us, length us, event | category | flops | bytes accessed | tf_op | source)
XLA Modules:
  0.0 73.7 jit_solution(9210836240859607534)
XLA Ops:
  0.6 71.9 %shard_map.59 = (f32[64,128]{1,0:T(8,128)S(1)}, f32[64,128]{1,0:T(8,128)S(1)}) custom-call(f32[64,128]{1,0:T(8,128)} %v0_in.1, f32[3,128]{1,0:T(4,128)} %geo_in.1, f32[1,128]{1,0:T(1,128)} %bitcast.1, s32[1,7]{1,0:T(1,128)} %own_in.1), custom_call_target="tpu_custom_call" | custom-call | tf_op jit(solution)/shard_map/pallas_call | solution.py:414
  72.5 0.6 copy.8
  73.1 0.6 copy.9
